TPU v7x, 256 devices: a whole 4x4x8 slice. The times are simulated.
256 devices in a mesh: mom: 4 (over y_hi, core), tr: 8 (over y_lo, x), tc: 8 (over z).
Axes of the slice: x: 4, y: 4 (y_hi: 2, y_lo: 2; y = y_hi * 2 + y_lo), z: 8, core: 2. Of those that a mesh axis runs over, the one named last changes fastest.
Arguments:
- start_rows: float32 [256, 8, 8192], P('tr', 'mom', 'tc'), may hold values from -6 to 6
- sigma_start: float32 [256, 8, 8192], P('tr', 'mom', 'tc'), may hold values from -6 to 6
- history: float32 [8, 8192, 8192], P('mom', 'tr', 'tc'), may hold values from -0.0625 to 0.0625
- interaction: float32 [2, 256, 8, 8192], P(None, 'tr', None, 'tc'), may hold values from -1.2 to 1.2
Outputs:
- first_rows: float32 [256, 8, 8192], P('tr', 'mom', 'tc')
- last_rows: float32 [256, 8, 8192], P('tr', 'mom', 'tc')
- last_sigma: float32 [256, 8, 8192], P('tr', 'mom', 'tc')
All inputs are finite; a program needn't handle non-finite values.
Results may differ from a plain program's by a relative error of at most 0.00011.
Values sent between devices are 32-bit elements; how exact they have to be, the bound alone decides.
No kernel may reach another device: no remote copies, remote signals or barrier semaphores. Data moves between devices by JAX's collectives and lax.ppermute only.
A program may use at most 128 MiB of HBM per device.

v0:
```python
import jax
import jax.numpy as jnp
from jax import lax
from jax.sharding import PartitionSpec as P

CORRECTORS = 2


def from_everyone(x, axis):
    copies = jnp.broadcast_to(x, (lax.axis_size(axis), *x.shape))
    return lax.all_to_all(copies, axis, split_axis=0, concat_axis=0, tiled=True)


def laid_out(blocks, dim):
    dims = list(blocks.shape[1:])
    dims[dim] *= blocks.shape[0]
    return jnp.moveaxis(blocks, 0, dim).reshape(dims)


def collect(x, axis, dim):
    blocks = from_everyone(x, axis)
    return laid_out(blocks, dim)


def split_up(x, dim, count):
    before, after = (x.shape[:dim], x.shape[dim + 1 :])
    return jnp.moveaxis(x.reshape(*before, count, -1, *after), dim, 0)


def cut_rows(length, count):
    unit = 8 if length >= 8 * count else 1
    return [length // unit * k // count * unit for k in range(1, count)]


def several_exchanges(x, axis, pieces, split_dim, concat_dim):
    blocks = split_up(x, split_dim, lax.axis_size(axis))
    cut = max(range(1, max(2, blocks.ndim - 1)), key=lambda d: blocks.shape[d])
    done = []
    for section in jnp.split(blocks, cut_rows(blocks.shape[cut], pieces), axis=cut):
        if section.size:
            done.append(lax.all_to_all(section, axis, split_axis=0, concat_axis=0, tiled=True))
    return laid_out(jnp.concatenate(done, axis=cut), concat_dim)


def sum_at_owner(x, axis, dim):
    blocks = split_up(x, dim, lax.axis_size(axis))
    arrived = lax.all_to_all(blocks, axis, split_axis=0, concat_axis=0, tiled=True)
    return arrived.sum(axis=0)


def relayout(energy):
    widened = collect(energy, "tc", 2)
    return several_exchanges(widened, "tr", 2, 2, 0)


def body(start_rows, sigma_start, history, interaction):
    groups = lax.axis_size("mom")
    local_count = start_rows.shape[1]
    total_count = local_count * groups
    group_index = lax.axis_index("mom")
    momenta = group_index * local_count + jnp.arange(local_count, dtype=jnp.int32)
    shifts = jnp.arange(total_count, dtype=jnp.int32)
    green = start_rows
    energy = sigma_start
    spread_energy = relayout(energy)
    block_total = interaction.shape[0]
    results = []
    for block_index in range(block_total):
        weights_now = interaction[block_index]
        base_rows = green
        for sweep_index in range(CORRECTORS):
            energy_piece = spread_energy
            green = base_rows + sum_at_owner(
                jnp.einsum(
                    "rmt,mtc->rmc",
                    energy_piece,
                    history,
                    precision=lax.Precision.HIGHEST,
                    preferred_element_type=jnp.float32,
                ),
                "tr",
                0,
            )
            every_green = collect(green, "mom", 1)
            wanted = jnp.mod(momenta[:, None] - shifts[None, :], total_count)
            select_table = (wanted[:, :, None] == shifts[None, None, :]).astype(jnp.float32)
            energy = jnp.einsum(
                "rdc,mdq,rqc->rmc",
                weights_now,
                select_table,
                every_green,
                precision=lax.Precision.HIGHEST,
            )
            if not (block_index == block_total - 1 and sweep_index == CORRECTORS - 1):
                spread_energy = relayout(energy)
        results.append(green)
    return (results[0], results[block_total - 1], energy)


def solution(mesh):
    return jax.shard_map(
        body,
        mesh=mesh,
        in_specs=(
            P("tr", "mom", "tc"),
            P("tr", "mom", "tc"),
            P("mom", "tr", "tc"),
            P(None, "tr", None, "tc"),
        ),
        out_specs=(P("tr", "mom", "tc"), P("tr", "mom", "tc"), P("tr", "mom", "tc")),
        check_vma=False,
    )
```

profile of v0, /device:TPU:1, one launch (start us, length us, event | category | flops | bytes accessed | tf_op | source)
XLA Modules:
  0.0 594.2 jit_solution(1170452479583945919)
XLA Ops:
  1.9 58.5 %all_to_all.100 = f32[8,32,2,1024]{3,1,2,0:T(8,128)S(1)} all-to-all(f32[8,32,2,1024]{3,1,2,0:T(8,128)S(1)} %broadcast_in_dim.16), channel_id=1, replica_groups=mesh['mom'=4,'tr'=8,'tc'=8] {'tc'}, dimensions={0} | all-to-all | bytes 4194304 | tf_op jit(solution)/shard_map/all_to_all | solution.py:11
  60.6 18.2 %all_to_all.101 = f32[8,16,2,1024]{3,1,2,0:T(8,128)S(1)} all-to-all(f32[8,16,2,1024]{3,1,2,0:T(8,128)S(1)} %get-tuple-element.12), channel_id=1, replica_groups=mesh['mom'=4,'tr'=8,'tc'=8] {'tr'}, dimensions={0} | all-to-all | bytes 2097152 | tf_op jit(solution)/shard_map/all_to_all | solution.py:41
  78.8 14.7 %all_to_all.102 = f32[8,16,2,1024]{3,1,2,0:T(8,128)S(1)} all-to-all(f32[8,16,2,1024]{3,1,2,0:T(8,128)S(1)} %get-tuple-element.13), channel_id=1, replica_groups=mesh['mom'=4,'tr'=8,'tc'=8] {'tr'}, dimensions={0} | all-to-all | bytes 2097152 | tf_op jit(solution)/shard_map/all_to_all | solution.py:41
  94.0 7.3 %fusion.16 = f32[2,256,1024]{2,1,0:T(8,128)S(1)} fusion(f32[256,2,1024]{2,0,1:T(8,128)S(1)} %bitcast.88, f32[2,1024,1024]{2,1,0:T(8,128)S(1)} %bitcast.81), kind=kOutput, calls=%fused_computation.30 | convolution fusion | flops 6442450944 | bytes 12582912 | tf_op jit(solution)/shard_map/rmt,mtc->rmc/dot_general | solution.py:74
  101.6 25.3 %all_to_all.103 = f32[8,32,2,1024]{3,1,2,0:T(8,128)S(1)} all-to-all(f32[8,32,2,1024]{3,1,2,0:T(8,128)S(1)} %copy.15), channel_id=1, replica_groups=mesh['mom'=4,'tr'=8,'tc'=8] {'tr'}, dimensions={0} | all-to-all | bytes 4194304 | tf_op jit(solution)/shard_map/all_to_all | solution.py:47
  129.1 9.3 %all-to-all-start.4 = ((f32[4,32,2,1024]{3,1,2,0:T(8,128)}), f32[4,32,2,1024]{3,1,2,0:T(8,128)S(1)}, u32[]{:S(2)}, u32[]{:S(2)}) async-start(f32[4,32,2,1024]{3,1,2,0:T(8,128)} %broadcast_in_dim.17), calls=%async_computation.4 | async-start | bytes 2097152 | tf_op jit(solution)/shard_map/all_to_all | solution.py:11
  138.5 15.0 %all-to-all-done.4 = f32[4,32,2,1024]{3,1,2,0:T(8,128)S(1)} async-done(((f32[4,32,2,1024]{3,1,2,0:T(8,128)}), f32[4,32,2,1024]{3,1,2,0:T(8,128)S(1)}, u32[]{:S(2)}, u32[]{:S(2)}) %all-to-all-start.4) | async-done | bytes 1048608 | tf_op jit(solution)/shard_map/all_to_all | solution.py:11
  157.2 54.7 %all_to_all.104 = f32[8,32,2,1024]{3,1,2,0:T(8,128)S(1)} all-to-all(f32[8,32,2,1024]{3,1,2,0:T(8,128)S(1)} %broadcast_in_dim.18), channel_id=1, replica_groups=mesh['mom'=4,'tr'=8,'tc'=8] {'tc'}, dimensions={0} | all-to-all | bytes 4194304 | tf_op jit(solution)/shard_map/all_to_all | solution.py:11
  212.1 15.8 %all_to_all.105 = f32[8,16,2,1024]{3,1,2,0:T(8,128)S(1)} all-to-all(f32[8,16,2,1024]{3,1,2,0:T(8,128)S(1)} %get-tuple-element.10), channel_id=1, replica_groups=mesh['mom'=4,'tr'=8,'tc'=8] {'tr'}, dimensions={0} | all-to-all | bytes 2097152 | tf_op jit(solution)/shard_map/all_to_all | solution.py:41
  227.9 14.9 %all_to_all.106 = f32[8,16,2,1024]{3,1,2,0:T(8,128)S(1)} all-to-all(f32[8,16,2,1024]{3,1,2,0:T(8,128)S(1)} %get-tuple-element.11), channel_id=1, replica_groups=mesh['mom'=4,'tr'=8,'tc'=8] {'tr'}, dimensions={0} | all-to-all | bytes 2097152 | tf_op jit(solution)/shard_map/all_to_all | solution.py:41
  243.3 7.3 %fusion.17 = f32[2,256,1024]{2,1,0:T(8,128)S(1)} fusion(f32[256,2,1024]{2,0,1:T(8,128)S(1)} %bitcast.90, f32[2,1024,1024]{2,1,0:T(8,128)S(1)} %bitcast.83), kind=kOutput, calls=%fused_computation.31 | convolution fusion | flops 6442450944 | bytes 12582912 | tf_op jit(solution)/shard_map/rmt,mtc->rmc/dot_general | solution.py:74
  250.9 25.3 %all_to_all.107 = f32[8,32,2,1024]{3,1,2,0:T(8,128)S(1)} all-to-all(f32[8,32,2,1024]{3,1,2,0:T(8,128)S(1)} %copy.19), channel_id=1, replica_groups=mesh['mom'=4,'tr'=8,'tc'=8] {'tr'}, dimensions={0} | all-to-all | bytes 4194304 | tf_op jit(solution)/shard_map/all_to_all | solution.py:47
  276.6 22.5 %all_to_all.108 = f32[4,32,2,1024]{3,1,2,0:T(8,128)S(1)} all-to-all(f32[4,32,2,1024]{3,1,2,0:T(8,128)S(1)} %broadcast_in_dim.19), channel_id=1, replica_groups=mesh['mom'=4,'tr'=8,'tc'=8] {'mom'}, dimensions={0} | all-to-all | bytes 2097152 | tf_op jit(solution)/shard_map/all_to_all | solution.py:11
  300.8 54.8 %all_to_all.109 = f32[8,32,2,1024]{3,1,2,0:T(8,128)S(1)} all-to-all(f32[8,32,2,1024]{3,1,2,0:T(8,128)S(1)} %broadcast_in_dim.20), channel_id=1, replica_groups=mesh['mom'=4,'tr'=8,'tc'=8] {'tc'}, dimensions={0} | all-to-all | bytes 4194304 | tf_op jit(solution)/shard_map/all_to_all | solution.py:11
  355.8 15.7 %all_to_all.110 = f32[8,16,2,1024]{3,1,2,0:T(8,128)S(1)} all-to-all(f32[8,16,2,1024]{3,1,2,0:T(8,128)S(1)} %get-tuple-element.8), channel_id=1, replica_groups=mesh['mom'=4,'tr'=8,'tc'=8] {'tr'}, dimensions={0} | all-to-all | bytes 2097152 | tf_op jit(solution)/shard_map/all_to_all | solution.py:41
  371.6 15.0 %all_to_all.111 = f32[8,16,2,1024]{3,1,2,0:T(8,128)S(1)} all-to-all(f32[8,16,2,1024]{3,1,2,0:T(8,128)S(1)} %get-tuple-element.9), channel_id=1, replica_groups=mesh['mom'=4,'tr'=8,'tc'=8] {'tr'}, dimensions={0} | all-to-all | bytes 2097152 | tf_op jit(solution)/shard_map/all_to_all | solution.py:41
  394.6 25.3 %all_to_all.112 = f32[8,32,2,1024]{3,1,2,0:T(8,128)S(1)} all-to-all(f32[8,32,2,1024]{3,1,2,0:T(8,128)S(1)} %copy.23), channel_id=1, replica_groups=mesh['mom'=4,'tr'=8,'tc'=8] {'tr'}, dimensions={0} | all-to-all | bytes 4194304 | tf_op jit(solution)/shard_map/all_to_all | solution.py:47
  420.3 23.0 %all_to_all.113 = f32[4,32,2,1024]{3,1,2,0:T(8,128)S(1)} all-to-all(f32[4,32,2,1024]{3,1,2,0:T(8,128)S(1)} %broadcast_in_dim.21), channel_id=1, replica_groups=mesh['mom'=4,'tr'=8,'tc'=8] {'mom'}, dimensions={0} | all-to-all | bytes 2097152 | tf_op jit(solution)/shard_map/all_to_all | solution.py:11
  446.9 54.5 %all_to_all.114 = f32[8,32,2,1024]{3,1,2,0:T(8,128)S(1)} all-to-all(f32[8,32,2,1024]{3,1,2,0:T(8,128)S(1)} %broadcast_in_dim.22), channel_id=1, replica_groups=mesh['mom'=4,'tr'=8,'tc'=8] {'tc'}, dimensions={0} | all-to-all | bytes 4194304 | tf_op jit(solution)/shard_map/all_to_all | solution.py:11
  501.6 15.7 %all_to_all.115 = f32[8,16,2,1024]{3,1,2,0:T(8,128)S(1)} all-to-all(f32[8,16,2,1024]{3,1,2,0:T(8,128)S(1)} %get-tuple-element.6), channel_id=1, replica_groups=mesh['mom'=4,'tr'=8,'tc'=8] {'tr'}, dimensions={0} | all-to-all | bytes 2097152 | tf_op jit(solution)/shard_map/all_to_all | solution.py:41
  517.4 15.0 %all_to_all.116 = f32[8,16,2,1024]{3,1,2,0:T(8,128)S(1)} all-to-all(f32[8,16,2,1024]{3,1,2,0:T(8,128)S(1)} %get-tuple-element.7), channel_id=1, replica_groups=mesh['mom'=4,'tr'=8,'tc'=8] {'tr'}, dimensions={0} | all-to-all | bytes 2097152 | tf_op jit(solution)/shard_map/all_to_all | solution.py:41
  540.5 25.3 %all_to_all.117 = f32[8,32,2,1024]{3,1,2,0:T(8,128)S(1)} all-to-all(f32[8,32,2,1024]{3,1,2,0:T(8,128)S(1)} %copy.26), channel_id=1, replica_groups=mesh['mom'=4,'tr'=8,'tc'=8] {'tr'}, dimensions={0} | all-to-all | bytes 4194304 | tf_op jit(solution)/shard_map/all_to_all | solution.py:47
  567.8 8.5 %all-to-all-start.19 = ((f32[4,32,2,1024]{3,1,2,0:T(8,128)}), f32[4,32,2,1024]{3,1,2,0:T(8,128)S(1)}, u32[]{:S(2)}, u32[]{:S(2)}) async-start(f32[4,32,2,1024]{3,1,2,0:T(8,128)} %broadcast_in_dim.23), calls=%async_computation.19 | async-start | bytes 2097152 | tf_op jit(solution)/shard_map/all_to_all | solution.py:11
  579.0 12.3 %all-to-all-done.19 = f32[4,32,2,1024]{3,1,2,0:T(8,128)S(1)} async-done(((f32[4,32,2,1024]{3,1,2,0:T(8,128)}), f32[4,32,2,1024]{3,1,2,0:T(8,128)S(1)}, u32[]{:S(2)}, u32[]{:S(2)}) %all-to-all-start.19) | async-done | bytes 1048608 | tf_op jit(solution)/shard_map/all_to_all | solution.py:11
  (80 shorter events, 38.7 us)
Async XLA Ops:
  60.4 33.6 %slice-start = ((s8[8388608]{0:T(1024)(128)(4,1)}), s8[4194304]{0:T(1024)(128)(4,1)S(1)}, s32[]{:S(2)}) async-start(s8[8388608]{0:T(1024)(128)(4,1)} %bitcast.80), calls=%async_computation.20 | async-start | bytes 8388608
  78.8 15.2 %slice-start.1 = ((s8[8388608]{0:T(1024)(128)(4,1)}), s8[4194304]{0:T(1024)(128)(4,1)S(1)}, s32[]{:S(2)}) async-start(s8[8388608]{0:T(1024)(128)(4,1)} %bitcast.80), calls=%async_computation.21 | async-start | bytes 8388608
  126.9 1.0 copy-start.5
  129.1 25.0 %copy-start.3 = (f32[2,32,8,1024]{3,2,1,0:T(8,128)S(1)}, f32[2,32,8,1024]{3,2,1,0:T(8,128)}, u32[]{:S(2)}) copy-start(f32[2,32,8,1024]{3,2,1,0:T(8,128)} %param.7) | copy-start | bytes 6291460
  129.1 24.4 %all-to-all-start.4 = ((f32[4,32,2,1024]{3,1,2,0:T(8,128)}), f32[4,32,2,1024]{3,1,2,0:T(8,128)S(1)}, u32[]{:S(2)}, u32[]{:S(2)}) async-start(f32[4,32,2,1024]{3,1,2,0:T(8,128)} %broadcast_in_dim.17), calls=%async_computation.4 | async-start | bytes 2097152 | tf_op jit(solution)/shard_map/all_to_all | solution.py:11
  211.9 31.4 %slice-start.2 = ((s8[8388608]{0:T(1024)(128)(4,1)}), s8[4194304]{0:T(1024)(128)(4,1)S(1)}, s32[]{:S(2)}) async-start(s8[8388608]{0:T(1024)(128)(4,1)} %bitcast.82), calls=%async_computation.22 | async-start | bytes 8388608
  227.9 15.4 %slice-start.3 = ((s8[8388608]{0:T(1024)(128)(4,1)}), s8[4194304]{0:T(1024)(128)(4,1)S(1)}, s32[]{:S(2)}) async-start(s8[8388608]{0:T(1024)(128)(4,1)} %bitcast.82), calls=%async_computation.23 | async-start | bytes 8388608
  276.6 23.1 %copy-start.1 = (f32[2,8,32,1024]{3,1,2,0:T(8,128)S(1)}, f32[2,8,32,1024]{3,1,2,0:T(8,128)}, u32[]{:S(2)}) copy-start(f32[2,8,32,1024]{3,1,2,0:T(8,128)} %get-tuple-element.15) | copy-start | bytes 6291460
  355.6 31.4 %slice-start.4 = ((s8[8388608]{0:T(1024)(128)(4,1)}), s8[4194304]{0:T(1024)(128)(4,1)S(1)}, s32[]{:S(2)}) async-start(s8[8388608]{0:T(1024)(128)(4,1)} %bitcast.84), calls=%async_computation.24 | async-start | bytes 8388608
  371.6 15.5 %slice-start.5 = ((s8[8388608]{0:T(1024)(128)(4,1)}), s8[4194304]{0:T(1024)(128)(4,1)S(1)}, s32[]{:S(2)}) async-start(s8[8388608]{0:T(1024)(128)(4,1)} %bitcast.84), calls=%async_computation.25 | async-start | bytes 8388608
  420.3 23.6 %copy-start.4 = (f32[2,32,8,1024]{3,2,1,0:T(8,128)S(1)}, f32[2,32,8,1024]{3,2,1,0:T(8,128)}, u32[]{:S(2)}) copy-start(f32[2,32,8,1024]{3,2,1,0:T(8,128)} %param.7) | copy-start | bytes 6291460
  501.4 31.4 %slice-start.6 = ((s8[8388608]{0:T(1024)(128)(4,1)}), s8[4194304]{0:T(1024)(128)(4,1)S(1)}, s32[]{:S(2)}) async-start(s8[8388608]{0:T(1024)(128)(4,1)} %bitcast.86), calls=%async_computation.26 | async-start | bytes 8388608
  517.4 15.5 %slice-start.7 = ((s8[8388608]{0:T(1024)(128)(4,1)}), s8[4194304]{0:T(1024)(128)(4,1)S(1)}, s32[]{:S(2)}) async-start(s8[8388608]{0:T(1024)(128)(4,1)} %bitcast.86), calls=%async_computation.27 | async-start | bytes 8388608
  566.0 0.7 copy-start.2
  567.8 23.6 %all-to-all-start.19 = ((f32[4,32,2,1024]{3,1,2,0:T(8,128)}), f32[4,32,2,1024]{3,1,2,0:T(8,128)S(1)}, u32[]{:S(2)}, u32[]{:S(2)}) async-start(f32[4,32,2,1024]{3,1,2,0:T(8,128)} %broadcast_in_dim.23), calls=%async_computation.19 | async-start | bytes 2097152 | tf_op jit(solution)/shard_map/all_to_all | solution.py:11
  576.3 15.7 %copy-start = (f32[2,8,32,1024]{3,1,2,0:T(8,128)S(1)}, f32[2,8,32,1024]{3,1,2,0:T(8,128)}, u32[]{:S(2)}) copy-start(f32[2,8,32,1024]{3,1,2,0:T(8,128)} %get-tuple-element.17) | copy-start | bytes 6291460
where the time goes:
time: 603 us; the launch traced here: 594 us
  blocking collectives  494 us (82%)
  matrix products  34.9 us (6%)
  waiting for transfers between devices  27.4 us (5%)
  starting transfers between devices  17.8 us (3%)
  local copies, waits for them, and re-layouts  14.7 us (2%)
    all_to_all x6, blocking collectives, from_everyone(): return lax.all_to_all(copies, axis, split_axis=0, concat_axis=0, tiled=True)  268 us
    all_to_all x8, blocking collectives, several_exchanges(): lax.all_to_all(section, axis, split_axis=0, concat_axis=0, tiled=True)  125 us
    all_to_all x4, blocking collectives, sum_at_owner(): lax.all_to_all(blocks, axis, split_axis=0, concat_axis=0, tiled=True)  101 us
    dot_general x4, matrix products, body(): jnp.einsum('rmt,mtc->rmc', energy_piece, history, precision=lax.Precision...  29.3 us
    all_to_all x2, waiting for transfers between devices, from_everyone(): return lax.all_to_all(copies, axis, split_axis=0, concat_axis=0, tiled=True)  27.4 us
    all_to_all x2, starting transfers between devices, from_everyone(): return lax.all_to_all(copies, axis, split_axis=0, concat_axis=0, tiled=True)  17.8 us
  transfers between devices with their start and end apart: 2, of which 2 were waited for; matrix products, arithmetic and copies ran while one was open for 0% of the time, Pallas kernels for 0%

commit v1 on v0

v1 whole, which is shorter than its diff:
```python
import jax
import jax.numpy as jnp
from jax import lax
from jax.sharding import PartitionSpec as P

CORRECTORS = 2
GROUPS = 1
ALL = ("mom", "tr", "tc")


def ring(size, step):
    return [(k, (k + step) % size) for k in range(size)]


def along_x(step):
    return [(y * 4 + x, y * 4 + (x + step) % 4) for y in range(2) for x in range(4)]


Y_PAIR = [(y * 4 + x, (1 - y) * 4 + x) for y in range(2) for x in range(4)]


def turn(flip):
    return [
        ((m * 8 + i) * 8 + j, ((m ^ flip) * 8 + j) * 8 + i)
        for i in range(8)
        for m in range(4)
        for j in range(8)
    ]


def pick(pieces, index):
    stacked = jnp.stack(pieces)
    return lax.dynamic_index_in_dim(stacked, index, 0, keepdims=False)


def by_xor(pieces, me):
    low = (me & 1) == 1
    high = (me & 2) == 2
    a, b, c, d = pieces
    a, b, c, d = (
        jnp.where(low, b, a),
        jnp.where(low, a, b),
        jnp.where(low, d, c),
        jnp.where(low, c, d),
    )
    return (
        jnp.where(high, c, a),
        jnp.where(high, d, b),
        jnp.where(high, a, c),
        jnp.where(high, b, d),
    )


def gather_tc(piece):
    up = down = piece
    ups, downs = [], []
    for _ in range(3):
        up = lax.ppermute(up, "tc", ring(8, 1))
        down = lax.ppermute(down, "tc", ring(8, -1))
        ups.append(up)
        downs.append(down)
    half = piece.shape[1] // 2
    far = jnp.concatenate(
        [
            lax.ppermute(up[:, :half], "tc", ring(8, 1)),
            lax.ppermute(down[:, half:], "tc", ring(8, -1)),
        ],
        axis=1,
    )
    return [piece, *downs, far, *ups[::-1]]


def sum_tr(partial, start, x, y, z):
    count, total, width = partial.shape
    blocks = partial.reshape(count, 8, total // 8, width)

    def block(yy, xx):
        return lax.dynamic_index_in_dim(blocks, (yy * 4 + xx % 4 - z) % 8, 1, keepdims=False)

    from_low = lax.ppermute(block(0, x + 2), "tr", along_x(1))
    from_high = lax.ppermute(block(1, x + 2), "tr", along_x(-1))
    to_high = jnp.stack([block(0, x + 1) + from_low, block(1, x + 1)])
    to_low = jnp.stack([block(0, x + 3), block(1, x + 3) + from_high])
    got_low = lax.ppermute(to_high, "tr", along_x(1))
    got_high = lax.ppermute(to_low, "tr", along_x(-1))
    sums = [block(half, x) + got_low[half] + got_high[half] for half in range(2)]
    other = jnp.where(y == 0, sums[1], sums[0])
    mine = jnp.where(y == 0, sums[0], sums[1])
    return start + mine + lax.ppermute(other, "tr", Y_PAIR)


def quarters(value):
    return jnp.split(value, 4, axis=2)


def convolve(weights, green, me):
    parts = by_xor(quarters(green), me)
    arrived = [parts[0]]
    for flip in range(1, 4):
        arrived.append(lax.ppermute(parts[flip], "mom", [(m, m ^ flip) for m in range(4)]))
    pairs = by_xor(arrived, me)
    rows = [pairs[k // 2][k % 2] for k in range(8)]
    energy = []
    for k in range(8):
        energy.append(sum(weights[d] * rows[(k - d) % 8] for d in range(8)))
    return by_xor([jnp.stack(energy[2 * p : 2 * p + 2]) for p in range(4)], me)


def body(start_rows, sigma_start, history, interaction):
    me = lax.axis_index("mom")
    place = lax.axis_index("tr")
    z = lax.axis_index("tc")
    x, y = place % 4, place // 4
    width = start_rows.shape[2] // 4
    weights = lax.dynamic_slice_in_dim(interaction, me * width, width, 3).transpose(0, 2, 1, 3)

    def split(value):
        return jnp.split(value, GROUPS, axis=1)

    green = split(start_rows.transpose(1, 0, 2))
    blocks = interaction.shape[0]
    weights = [split(weights[b]) for b in range(blocks)]
    spread = [lax.ppermute(e, ALL, turn(0)) for e in split(sigma_start.transpose(1, 0, 2))]
    results = []
    for b in range(blocks):
        base = green
        for sweep in range(CORRECTORS):
            last = b == blocks - 1 and sweep == CORRECTORS - 1
            green, following = [], []
            for g in range(GROUPS):
                gathered = jnp.concatenate(gather_tc(spread[g]), axis=1)
                partial = jnp.einsum(
                    "mrt,mtc->mrc",
                    gathered,
                    history,
                    precision=lax.Precision.HIGH,
                    preferred_element_type=jnp.float32,
                )
                rows = sum_tr(partial, base[g], x, y, z)
                green.append(rows)
                parts = convolve(weights[b][g], rows, me)
                if last:
                    back = [parts[0]] + [
                        lax.ppermute(parts[f], "mom", [(m, m ^ f) for m in range(4)])
                        for f in range(1, 4)
                    ]
                else:
                    back = [lax.ppermute(parts[f], ALL, turn(f)) for f in range(4)]
                following.append(jnp.concatenate(by_xor(back, me), axis=2))
            spread = following
        results.append(green)

    def whole(groups):
        return jnp.concatenate(groups, axis=1).transpose(1, 0, 2)

    return whole(results[0]), whole(results[-1]), whole(spread)


def solution(mesh):
    return jax.shard_map(
        body,
        mesh=mesh,
        in_specs=(
            P("tr", "mom", "tc"),
            P("tr", "mom", "tc"),
            P("mom", "tr", "tc"),
            P(None, "tr", None, "tc"),
        ),
        out_specs=(P("tr", "mom", "tc"), P("tr", "mom", "tc"), P("tr", "mom", "tc")),
        check_vma=False,
    )
```

time: 603 us -> 441 us (0.73)
  blocking collectives: 494 us -> 0 us
  starting transfers between devices: 17.8 us -> 226 us
  waiting for transfers between devices: 27.4 us -> 169 us
  matrix products: 34.9 us -> 19.8 us
  local copies, waits for them, and re-layouts: 14.7 us -> 7.33 us
    all_to_all x18 -> x0, blocking collectives: 494 us -> none  [the longest x6 268 us: from_everyone(): return lax.all_to_all(copies, axis, split_axis=0, concat_axis=0, tiled=True)]
    ppermute x0 -> x80, starting transfers between devices: none -> 226 us  [the longest x12 96.7 us: gather_tc(): up = lax.ppermute(up, 'tc', ring(8, 1))]
    ppermute x0 -> x80, waiting for transfers between devices: none -> 169 us  [the longest x12 58.8 us: gather_tc(): up = lax.ppermute(up, 'tc', ring(8, 1))]
    all_to_all x2 -> x0, waiting for transfers between devices: 27.4 us -> none  [from_everyone(): return lax.all_to_all(copies, axis, split_axis=0, concat_axis=0, tiled=True)]
    all_to_all x2 -> x0, starting transfers between devices: 17.8 us -> none  [from_everyone(): return lax.all_to_all(copies, axis, split_axis=0, concat_axis=0, tiled=True)]
    dot_general x6 -> x4, matrix products: 34.9 us -> 19.8 us  [body(): jnp.einsum('mrt,mtc->mrc', gathered, history, precision=lax.Precision.HIG...]
  transfers between devices with their start and end apart: 2 -> 80, of which waited for: 2 -> 50; matrix products, arithmetic and copies ran while one was open for 0% -> 1% of each run, Pallas kernels for 0% -> 0%
where the time goes in v1:
time: 441 us; the launch traced here: 432 us
  starting transfers between devices  226 us (51%)
  waiting for transfers between devices  169 us (38%)
  matrix products  19.8 us (4%)
  other arithmetic  8.05 us (2%)
  local copies, waits for them, and re-layouts  7.33 us (2%)
    ppermute x12, starting transfers between devices, gather_tc(): up = lax.ppermute(up, 'tc', ring(8, 1))  96.7 us
    ppermute x12, waiting for transfers between devices, gather_tc(): up = lax.ppermute(up, 'tc', ring(8, 1))  58.8 us
    ppermute x12, starting transfers between devices, convolve(): lax.ppermute(parts[flip], 'mom', [(m, m ^ flip) for m in range(4)])  43.7 us
    ppermute x12, starting transfers between devices, gather_tc(): down = lax.ppermute(down, 'tc', ring(8, -1))  30 us
    ppermute x4, waiting for transfers between devices, sum_tr(): got_low = lax.ppermute(to_high, 'tr', along_x(1))  27.3 us
    ppermute x4, waiting for transfers between devices, sum_tr(): return start + mine + lax.ppermute(other, 'tr', Y_PAIR)  21.1 us
    dot_general x4, matrix products, body(): jnp.einsum('mrt,mtc->mrc', gathered, history, precision=lax.Precision.HIG...  19.8 us
    ppermute x12, waiting for transfers between devices, convolve(): lax.ppermute(parts[flip], 'mom', [(m, m ^ flip) for m in range(4)])  15.9 us
  transfers between devices with their start and end apart: 80, of which 50 were waited for; matrix products, arithmetic and copies ran while one was open for 1% of the time, Pallas kernels for 0%

profile of v1, /device:TPU:1, one launch (start us, length us, event | category | flops | bytes accessed | tf_op | source)
XLA Modules:
  0.0 432.2 jit_solution(17861930900529370876)
XLA Ops:
  2.5 28.7 %collective-permute-start.4 = (f32[2,32,1024]{2,1,0:T(8,128)S(1)}, f32[2,32,1024]{2,1,0:T(8,128)S(1)}, u32[]{:S(2)}, u32[]{:S(2)}) collective-permute-start(f32[2,32,1024]{2,1,0:T(8,128)S(1)} %collective-permute-done), channel_id=1, source_target_pairs={{0,1},{1,2},{2,3},{3,4},{4,5},{5,6},{6,7},{7,0},{8,9},{9,10},{10,1... | collective-permute-start | bytes 786440 | tf_op jit(solution)/shard_map/ppermute | solution.py:58
  60.6 6.3 %fusion.52 = f32[2,256,1024]{2,1,0:T(8,128)S(1)} fusion(f32[2,256,1024]{2,1,0:T(8,128)S(1)} %constant_dynamic-update-slice_fusion, f32[2,1024,1024]{2,1,0:T(8,128)} %param.6), kind=kOutput, calls=%fused_computation.317 | convolution fusion | flops 3221225472 | bytes 12582912 | tf_op jit(solution)/shard_map/mrt,mtc->mrc/dot_general | solution.py:132
  69.3 5.2 %collective-permute-start.9 = (f32[2,32,1024]{2,1,0:T(8,128)S(1)}, f32[2,32,1024]{2,1,0:T(8,128)}, u32[]{:S(2)}, u32[]{:S(2)}) collective-permute-start(f32[2,32,1024]{2,1,0:T(8,128)S(1)} %get-tuple-element.53), channel_id=1, source_target_pairs={{0,8},{8,16},{16,24},{24,0},{32,40},{40,48},{48,56},{56,32},{1,9},... | collective-permute-start | bytes 786440 | tf_op jit(solution)/shard_map/ppermute | solution.py:80
  85.7 6.3 %collective-permute-done.10 = f32[2,2,32,1024]{3,2,1,0:T(8,128)S(1)} collective-permute-done((f32[2,2,32,1024]{3,2,1,0:T(8,128)}, f32[2,2,32,1024]{3,2,1,0:T(8,128)S(1)}, u32[]{:S(2)}, u32[]{:S(2)}) %collective-permute-start.10) | collective-permute-done | bytes 524320 | tf_op jit(solution)/shard_map/ppermute | solution.py:84
  94.4 5.4 %collective-permute-done.13 = f32[2,32,1024]{2,1,0:T(8,128)S(1)} collective-permute-done((f32[2,32,1024]{2,1,0:T(8,128)}, f32[2,32,1024]{2,1,0:T(8,128)S(1)}, u32[]{:S(2)}, u32[]{:S(2)}) %collective-permute-start.13) | collective-permute-done | bytes 262176 | tf_op jit(solution)/shard_map/ppermute | solution.py:89
  100.0 13.0 %collective-permute-start.14 = (f32[2,32,256]{2,1,0:T(8,128)S(1)}, f32[2,32,256]{2,1,0:T(8,128)S(1)}, u32[]{:S(2)}, u32[]{:S(2)}) collective-permute-start(f32[2,32,256]{2,1,0:T(8,128)S(1)} %get-tuple-element.125), channel_id=1, source_target_pairs={{0,192},{64,128},{128,64},{192,0},{1,193},{65,129},{129,65},{193,1... | collective-permute-start | bytes 196616 | tf_op jit(solution)/shard_map/ppermute | solution.py:100
  126.8 20.8 %collective-permute-start.24 = (f32[2,32,1024]{2,1,0:T(8,128)S(1)}, f32[2,32,1024]{2,1,0:T(8,128)S(1)}, u32[]{:S(2)}, u32[]{:S(2)}) collective-permute-start(f32[2,32,1024]{2,1,0:T(8,128)S(1)} %get-tuple-element.114), channel_id=1, source_target_pairs={{0,1},{1,2},{2,3},{3,4},{4,5},{5,6},{6,7},{7,0},{8,9},{9,10},{10,1... | collective-permute-start | bytes 786440 | tf_op jit(solution)/shard_map/ppermute | solution.py:58
  151.1 6.3 %collective-permute-done.24 = f32[2,32,1024]{2,1,0:T(8,128)S(1)} collective-permute-done((f32[2,32,1024]{2,1,0:T(8,128)S(1)}, f32[2,32,1024]{2,1,0:T(8,128)S(1)}, u32[]{:S(2)}, u32[]{:S(2)}) %collective-permute-start.24) | collective-permute-done | bytes 262176 | tf_op jit(solution)/shard_map/ppermute | solution.py:58
  160.0 5.4 %collective-permute-done.25 = f32[2,32,1024]{2,1,0:T(8,128)S(1)} collective-permute-done((f32[2,32,1024]{2,1,0:T(8,128)S(1)}, f32[2,32,1024]{2,1,0:T(8,128)S(1)}, u32[]{:S(2)}, u32[]{:S(2)}) %collective-permute-start.25) | collective-permute-done | bytes 262176 | tf_op jit(solution)/shard_map/ppermute | solution.py:58
  192.1 6.9 %collective-permute-done.30 = f32[2,2,32,1024]{3,2,1,0:T(8,128)S(1)} collective-permute-done((f32[2,2,32,1024]{3,2,1,0:T(8,128)S(1)}, f32[2,2,32,1024]{3,2,1,0:T(8,128)S(1)}, u32[]{:S(2)}, u32[]{:S(2)}) %collective-permute-start.30) | collective-permute-done | bytes 524320 | tf_op jit(solution)/shard_map/ppermute | solution.py:84
  199.9 4.9 %collective-permute-done.33 = f32[2,32,1024]{2,1,0:T(8,128)S(1)} collective-permute-done((f32[2,32,1024]{2,1,0:T(8,128)S(1)}, f32[2,32,1024]{2,1,0:T(8,128)S(1)}, u32[]{:S(2)}, u32[]{:S(2)}) %collective-permute-start.33) | collective-permute-done | bytes 262176 | tf_op jit(solution)/shard_map/ppermute | solution.py:89
  205.0 9.4 %collective-permute-start.34 = (f32[2,32,256]{2,1,0:T(8,128)S(1)}, f32[2,32,256]{2,1,0:T(8,128)S(1)}, u32[]{:S(2)}, u32[]{:S(2)}) collective-permute-start(f32[2,32,256]{2,1,0:T(8,128)S(1)} %get-tuple-element.110), channel_id=1, source_target_pairs={{0,192},{64,128},{128,64},{192,0},{1,193},{65,129},{129,65},{193,1... | collective-permute-start | bytes 196616 | tf_op jit(solution)/shard_map/ppermute | solution.py:100
  228.1 21.4 %collective-permute-start.44 = (f32[2,32,1024]{2,1,0:T(8,128)S(1)}, f32[2,32,1024]{2,1,0:T(8,128)S(1)}, u32[]{:S(2)}, u32[]{:S(2)}) collective-permute-start(f32[2,32,1024]{2,1,0:T(8,128)S(1)} %get-tuple-element.99), channel_id=1, source_target_pairs={{0,1},{1,2},{2,3},{3,4},{4,5},{5,6},{6,7},{7,0},{8,9},{9,10},{10,1... | collective-permute-start | bytes 786440 | tf_op jit(solution)/shard_map/ppermute | solution.py:58
  252.9 6.3 %collective-permute-done.44 = f32[2,32,1024]{2,1,0:T(8,128)S(1)} collective-permute-done((f32[2,32,1024]{2,1,0:T(8,128)S(1)}, f32[2,32,1024]{2,1,0:T(8,128)S(1)}, u32[]{:S(2)}, u32[]{:S(2)}) %collective-permute-start.44) | collective-permute-done | bytes 262176 | tf_op jit(solution)/shard_map/ppermute | solution.py:58
  261.9 5.4 %collective-permute-done.45 = f32[2,32,1024]{2,1,0:T(8,128)S(1)} collective-permute-done((f32[2,32,1024]{2,1,0:T(8,128)S(1)}, f32[2,32,1024]{2,1,0:T(8,128)S(1)}, u32[]{:S(2)}, u32[]{:S(2)}) %collective-permute-start.45) | collective-permute-done | bytes 262176 | tf_op jit(solution)/shard_map/ppermute | solution.py:58
  294.1 7.2 %collective-permute-done.50 = f32[2,2,32,1024]{3,2,1,0:T(8,128)S(1)} collective-permute-done((f32[2,2,32,1024]{3,2,1,0:T(8,128)S(1)}, f32[2,2,32,1024]{3,2,1,0:T(8,128)S(1)}, u32[]{:S(2)}, u32[]{:S(2)}) %collective-permute-start.50) | collective-permute-done | bytes 524320 | tf_op jit(solution)/shard_map/ppermute | solution.py:84
  301.5 5.3 %collective-permute-done.53 = f32[2,32,1024]{2,1,0:T(8,128)S(1)} collective-permute-done((f32[2,32,1024]{2,1,0:T(8,128)S(1)}, f32[2,32,1024]{2,1,0:T(8,128)S(1)}, u32[]{:S(2)}, u32[]{:S(2)}) %collective-permute-start.53) | collective-permute-done | bytes 262176 | tf_op jit(solution)/shard_map/ppermute | solution.py:89
  306.8 9.3 %collective-permute-start.54 = (f32[2,32,256]{2,1,0:T(8,128)S(1)}, f32[2,32,256]{2,1,0:T(8,128)S(1)}, u32[]{:S(2)}, u32[]{:S(2)}) collective-permute-start(f32[2,32,256]{2,1,0:T(8,128)S(1)} %get-tuple-element.95), channel_id=1, source_target_pairs={{0,192},{64,128},{128,64},{192,0},{1,193},{65,129},{129,65},{193,1... | collective-permute-start | bytes 196616 | tf_op jit(solution)/shard_map/ppermute | solution.py:100
  329.9 20.8 %collective-permute-start.64 = (f32[2,32,1024]{2,1,0:T(8,128)S(1)}, f32[2,32,1024]{2,1,0:T(8,128)S(1)}, u32[]{:S(2)}, u32[]{:S(2)}) collective-permute-start(f32[2,32,1024]{2,1,0:T(8,128)S(1)} %get-tuple-element.84), channel_id=1, source_target_pairs={{0,1},{1,2},{2,3},{3,4},{4,5},{5,6},{6,7},{7,0},{8,9},{9,10},{10,1... | collective-permute-start | bytes 786440 | tf_op jit(solution)/shard_map/ppermute | solution.py:58
  354.6 6.3 %collective-permute-done.64 = f32[2,32,1024]{2,1,0:T(8,128)S(1)} collective-permute-done((f32[2,32,1024]{2,1,0:T(8,128)S(1)}, f32[2,32,1024]{2,1,0:T(8,128)S(1)}, u32[]{:S(2)}, u32[]{:S(2)}) %collective-permute-start.64) | collective-permute-done | bytes 262176 | tf_op jit(solution)/shard_map/ppermute | solution.py:58
  363.5 5.4 %collective-permute-done.65 = f32[2,32,1024]{2,1,0:T(8,128)S(1)} collective-permute-done((f32[2,32,1024]{2,1,0:T(8,128)S(1)}, f32[2,32,1024]{2,1,0:T(8,128)S(1)}, u32[]{:S(2)}, u32[]{:S(2)}) %collective-permute-start.65) | collective-permute-done | bytes 262176 | tf_op jit(solution)/shard_map/ppermute | solution.py:58
  395.5 6.9 %collective-permute-done.70 = f32[2,2,32,1024]{3,2,1,0:T(8,128)S(1)} collective-permute-done((f32[2,2,32,1024]{3,2,1,0:T(8,128)S(1)}, f32[2,2,32,1024]{3,2,1,0:T(8,128)S(1)}, u32[]{:S(2)}, u32[]{:S(2)}) %collective-permute-start.70) | collective-permute-done | bytes 524320 | tf_op jit(solution)/shard_map/ppermute | solution.py:84
  402.7 5.5 %collective-permute-done.73 = f32[2,32,1024]{2,1,0:T(8,128)S(1)} collective-permute-done((f32[2,32,1024]{2,1,0:T(8,128)S(1)}, f32[2,32,1024]{2,1,0:T(8,128)S(1)}, u32[]{:S(2)}, u32[]{:S(2)}) %collective-permute-start.73) | collective-permute-done | bytes 262176 | tf_op jit(solution)/shard_map/ppermute | solution.py:89
  408.3 9.5 %collective-permute-start.74 = (f32[2,32,256]{2,1,0:T(8,128)S(1)}, f32[2,32,256]{2,1,0:T(8,128)S(1)}, u32[]{:S(2)}, u32[]{:S(2)}) collective-permute-start(f32[2,32,256]{2,1,0:T(8,128)S(1)} %get-tuple-element.80), channel_id=1, source_target_pairs={{0,192},{64,128},{128,64},{192,0},{1,193},{65,129},{129,65},{193,1... | collective-permute-start | bytes 196616 | tf_op jit(solution)/shard_map/ppermute | solution.py:100
  (280 shorter events, 202.1 us)
Async XLA Ops:
  2.5 35.1 %collective-permute-start.4 = (f32[2,32,1024]{2,1,0:T(8,128)S(1)}, f32[2,32,1024]{2,1,0:T(8,128)S(1)}, u32[]{:S(2)}, u32[]{:S(2)}) collective-permute-start(f32[2,32,1024]{2,1,0:T(8,128)S(1)} %collective-permute-done), channel_id=1, source_target_pairs={{0,1},{1,2},{2,3},{3,4},{4,5},{5,6},{6,7},{7,0},{8,9},{9,10},{10,1... | collective-permute-start | bytes 786440 | tf_op jit(solution)/shard_map/ppermute | solution.py:58
  31.3 9.8 %collective-permute-start.1 = (f32[2,32,1024]{2,1,0:T(8,128)S(1)}, f32[2,32,1024]{2,1,0:T(8,128)S(1)}, u32[]{:S(2)}, u32[]{:S(2)}) collective-permute-start(f32[2,32,1024]{2,1,0:T(8,128)S(1)} %collective-permute-done), channel_id=1, source_target_pairs={{0,7},{1,0},{2,1},{3,2},{4,3},{5,4},{6,5},{7,6},{8,15},{9,8},{10,9... | collective-permute-start | bytes 786440 | tf_op jit(solution)/shard_map/ppermute | solution.py:59
  68.3 9.8 %collective-permute-start.11 = (f32[2,32,1024]{2,1,0:T(8,128)S(1)}, f32[2,32,1024]{2,1,0:T(8,128)S(1)}, u32[]{:S(2)}, u32[]{:S(2)}) collective-permute-start(f32[2,32,1024]{2,1,0:T(8,128)S(1)} %get-tuple-element.54), channel_id=1, source_target_pairs={{0,24},{8,0},{16,8},{24,16},{32,56},{40,32},{48,40},{56,48},{1,25}... | collective-permute-start | bytes 786440 | tf_op jit(solution)/shard_map/ppermute | solution.py:81
  69.3 10.6 %collective-permute-start.9 = (f32[2,32,1024]{2,1,0:T(8,128)S(1)}, f32[2,32,1024]{2,1,0:T(8,128)}, u32[]{:S(2)}, u32[]{:S(2)}) collective-permute-start(f32[2,32,1024]{2,1,0:T(8,128)S(1)} %get-tuple-element.53), channel_id=1, source_target_pairs={{0,8},{8,16},{16,24},{24,0},{32,40},{40,48},{48,56},{56,32},{1,9},... | collective-permute-start | bytes 786440 | tf_op jit(solution)/shard_map/ppermute | solution.py:80
  81.9 10.0 %collective-permute-start.10 = (f32[2,2,32,1024]{3,2,1,0:T(8,128)}, f32[2,2,32,1024]{3,2,1,0:T(8,128)S(1)}, u32[]{:S(2)}, u32[]{:S(2)}) collective-permute-start(f32[2,2,32,1024]{3,2,1,0:T(8,128)} %pad_maximum_fusion), channel_id=1, source_target_pairs={{0,8},{8,16},{16,24},{24,0},{32,40},{40,48},{48,56},{56,32},{1,9},... | collective-permute-start | bytes 1572872 | tf_op jit(solution)/shard_map/ppermute | solution.py:84
  82.8 9.3 %collective-permute-start.12 = (f32[2,2,32,1024]{3,2,1,0:T(8,128)}, f32[2,2,32,1024]{3,2,1,0:T(8,128)}, u32[]{:S(2)}, u32[]{:S(2)}) collective-permute-start(f32[2,2,32,1024]{3,2,1,0:T(8,128)} %pad_maximum_fusion.1), channel_id=1, source_target_pairs={{0,24},{8,0},{16,8},{24,16},{32,56},{40,32},{48,40},{56,48},{1,25}... | collective-permute-start | bytes 1572872 | tf_op jit(solution)/shard_map/ppermute | solution.py:85
  100.0 15.0 %collective-permute-start.14 = (f32[2,32,256]{2,1,0:T(8,128)S(1)}, f32[2,32,256]{2,1,0:T(8,128)S(1)}, u32[]{:S(2)}, u32[]{:S(2)}) collective-permute-start(f32[2,32,256]{2,1,0:T(8,128)S(1)} %get-tuple-element.125), channel_id=1, source_target_pairs={{0,192},{64,128},{128,64},{192,0},{1,193},{65,129},{129,65},{193,1... | collective-permute-start | bytes 196616 | tf_op jit(solution)/shard_map/ppermute | solution.py:100
  126.8 30.5 %collective-permute-start.24 = (f32[2,32,1024]{2,1,0:T(8,128)S(1)}, f32[2,32,1024]{2,1,0:T(8,128)S(1)}, u32[]{:S(2)}, u32[]{:S(2)}) collective-permute-start(f32[2,32,1024]{2,1,0:T(8,128)S(1)} %get-tuple-element.114), channel_id=1, source_target_pairs={{0,1},{1,2},{2,3},{3,4},{4,5},{5,6},{6,7},{7,0},{8,9},{9,10},{10,1... | collective-permute-start | bytes 786440 | tf_op jit(solution)/shard_map/ppermute | solution.py:58
  147.6 9.7 %collective-permute-start.21 = (f32[2,32,1024]{2,1,0:T(8,128)S(1)}, f32[2,32,1024]{2,1,0:T(8,128)S(1)}, u32[]{:S(2)}, u32[]{:S(2)}) collective-permute-start(f32[2,32,1024]{2,1,0:T(8,128)S(1)} %get-tuple-element.114), channel_id=1, source_target_pairs={{0,7},{1,0},{2,1},{3,2},{4,3},{5,4},{6,5},{7,6},{8,15},{9,8},{10,9... | collective-permute-start | bytes 786440 | tf_op jit(solution)/shard_map/ppermute | solution.py:59
  157.3 8.1 %collective-permute-start.25 = (f32[2,32,1024]{2,1,0:T(8,128)S(1)}, f32[2,32,1024]{2,1,0:T(8,128)S(1)}, u32[]{:S(2)}, u32[]{:S(2)}) collective-permute-start(f32[2,32,1024]{2,1,0:T(8,128)S(1)} %collective-permute-done.24), channel_id=1, source_target_pairs={{0,1},{1,2},{2,3},{3,4},{4,5},{5,6},{6,7},{7,0},{8,9},{9,10},{10,1... | collective-permute-start | bytes 786440 | tf_op jit(solution)/shard_map/ppermute | solution.py:58
  189.3 9.8 %collective-permute-start.30 = (f32[2,2,32,1024]{3,2,1,0:T(8,128)S(1)}, f32[2,2,32,1024]{3,2,1,0:T(8,128)S(1)}, u32[]{:S(2)}, u32[]{:S(2)}) collective-permute-start(f32[2,2,32,1024]{3,2,1,0:T(8,128)S(1)} %pad_maximum_fusion.2), channel_id=1, source_target_pairs={{0,8},{8,16},{16,24},{24,0},{32,40},{40,48},{48,56},{56,32},{1,9},... | collective-permute-start | bytes 1572872 | tf_op jit(solution)/shard_map/ppermute | solution.py:84
  189.4 9.7 %collective-permute-start.32 = (f32[2,2,32,1024]{3,2,1,0:T(8,128)S(1)}, f32[2,2,32,1024]{3,2,1,0:T(8,128)S(1)}, u32[]{:S(2)}, u32[]{:S(2)}) collective-permute-start(f32[2,2,32,1024]{3,2,1,0:T(8,128)S(1)} %pad_maximum_fusion.3), channel_id=1, source_target_pairs={{0,24},{8,0},{16,8},{24,16},{32,56},{40,32},{48,40},{56,48},{1,25}... | collective-permute-start | bytes 1572872 | tf_op jit(solution)/shard_map/ppermute | solution.py:85
  205.0 12.0 %collective-permute-start.34 = (f32[2,32,256]{2,1,0:T(8,128)S(1)}, f32[2,32,256]{2,1,0:T(8,128)S(1)}, u32[]{:S(2)}, u32[]{:S(2)}) collective-permute-start(f32[2,32,256]{2,1,0:T(8,128)S(1)} %get-tuple-element.110), channel_id=1, source_target_pairs={{0,192},{64,128},{128,64},{192,0},{1,193},{65,129},{129,65},{193,1... | collective-permute-start | bytes 196616 | tf_op jit(solution)/shard_map/ppermute | solution.py:100
  228.1 31.1 %collective-permute-start.44 = (f32[2,32,1024]{2,1,0:T(8,128)S(1)}, f32[2,32,1024]{2,1,0:T(8,128)S(1)}, u32[]{:S(2)}, u32[]{:S(2)}) collective-permute-start(f32[2,32,1024]{2,1,0:T(8,128)S(1)} %get-tuple-element.99), channel_id=1, source_target_pairs={{0,1},{1,2},{2,3},{3,4},{4,5},{5,6},{6,7},{7,0},{8,9},{9,10},{10,1... | collective-permute-start | bytes 786440 | tf_op jit(solution)/shard_map/ppermute | solution.py:58
  249.5 9.7 %collective-permute-start.41 = (f32[2,32,1024]{2,1,0:T(8,128)S(1)}, f32[2,32,1024]{2,1,0:T(8,128)S(1)}, u32[]{:S(2)}, u32[]{:S(2)}) collective-permute-start(f32[2,32,1024]{2,1,0:T(8,128)S(1)} %get-tuple-element.99), channel_id=1, source_target_pairs={{0,7},{1,0},{2,1},{3,2},{4,3},{5,4},{6,5},{7,6},{8,15},{9,8},{10,9... | collective-permute-start | bytes 786440 | tf_op jit(solution)/shard_map/ppermute | solution.py:59
  259.2 8.1 %collective-permute-start.45 = (f32[2,32,1024]{2,1,0:T(8,128)S(1)}, f32[2,32,1024]{2,1,0:T(8,128)S(1)}, u32[]{:S(2)}, u32[]{:S(2)}) collective-permute-start(f32[2,32,1024]{2,1,0:T(8,128)S(1)} %collective-permute-done.44), channel_id=1, source_target_pairs={{0,1},{1,2},{2,3},{3,4},{4,5},{5,6},{6,7},{7,0},{8,9},{9,10},{10,1... | collective-permute-start | bytes 786440 | tf_op jit(solution)/shard_map/ppermute | solution.py:58
  291.0 10.3 %collective-permute-start.50 = (f32[2,2,32,1024]{3,2,1,0:T(8,128)S(1)}, f32[2,2,32,1024]{3,2,1,0:T(8,128)S(1)}, u32[]{:S(2)}, u32[]{:S(2)}) collective-permute-start(f32[2,2,32,1024]{3,2,1,0:T(8,128)S(1)} %pad_maximum_fusion.4), channel_id=1, source_target_pairs={{0,8},{8,16},{16,24},{24,0},{32,40},{40,48},{48,56},{56,32},{1,9},... | collective-permute-start | bytes 1572872 | tf_op jit(solution)/shard_map/ppermute | solution.py:84
  291.1 10.1 %collective-permute-start.52 = (f32[2,2,32,1024]{3,2,1,0:T(8,128)S(1)}, f32[2,2,32,1024]{3,2,1,0:T(8,128)S(1)}, u32[]{:S(2)}, u32[]{:S(2)}) collective-permute-start(f32[2,2,32,1024]{3,2,1,0:T(8,128)S(1)} %pad_maximum_fusion.5), channel_id=1, source_target_pairs={{0,24},{8,0},{16,8},{24,16},{32,56},{40,32},{48,40},{56,48},{1,25}... | collective-permute-start | bytes 1572872 | tf_op jit(solution)/shard_map/ppermute | solution.py:85
  306.8 12.0 %collective-permute-start.54 = (f32[2,32,256]{2,1,0:T(8,128)S(1)}, f32[2,32,256]{2,1,0:T(8,128)S(1)}, u32[]{:S(2)}, u32[]{:S(2)}) collective-permute-start(f32[2,32,256]{2,1,0:T(8,128)S(1)} %get-tuple-element.95), channel_id=1, source_target_pairs={{0,192},{64,128},{128,64},{192,0},{1,193},{65,129},{129,65},{193,1... | collective-permute-start | bytes 196616 | tf_op jit(solution)/shard_map/ppermute | solution.py:100
  329.9 30.9 %collective-permute-start.64 = (f32[2,32,1024]{2,1,0:T(8,128)S(1)}, f32[2,32,1024]{2,1,0:T(8,128)S(1)}, u32[]{:S(2)}, u32[]{:S(2)}) collective-permute-start(f32[2,32,1024]{2,1,0:T(8,128)S(1)} %get-tuple-element.84), channel_id=1, source_target_pairs={{0,1},{1,2},{2,3},{3,4},{4,5},{5,6},{6,7},{7,0},{8,9},{9,10},{10,1... | collective-permute-start | bytes 786440 | tf_op jit(solution)/shard_map/ppermute | solution.py:58
  350.7 10.2 %collective-permute-start.61 = (f32[2,32,1024]{2,1,0:T(8,128)S(1)}, f32[2,32,1024]{2,1,0:T(8,128)S(1)}, u32[]{:S(2)}, u32[]{:S(2)}) collective-permute-start(f32[2,32,1024]{2,1,0:T(8,128)S(1)} %get-tuple-element.84), channel_id=1, source_target_pairs={{0,7},{1,0},{2,1},{3,2},{4,3},{5,4},{6,5},{7,6},{8,15},{9,8},{10,9... | collective-permute-start | bytes 786440 | tf_op jit(solution)/shard_map/ppermute | solution.py:59
  392.6 9.8 %collective-permute-start.70 = (f32[2,2,32,1024]{3,2,1,0:T(8,128)S(1)}, f32[2,2,32,1024]{3,2,1,0:T(8,128)S(1)}, u32[]{:S(2)}, u32[]{:S(2)}) collective-permute-start(f32[2,2,32,1024]{3,2,1,0:T(8,128)S(1)} %pad_maximum_fusion.6), channel_id=1, source_target_pairs={{0,8},{8,16},{16,24},{24,0},{32,40},{40,48},{48,56},{56,32},{1,9},... | collective-permute-start | bytes 1572872 | tf_op jit(solution)/shard_map/ppermute | solution.py:84
  392.8 9.7 %collective-permute-start.72 = (f32[2,2,32,1024]{3,2,1,0:T(8,128)S(1)}, f32[2,2,32,1024]{3,2,1,0:T(8,128)S(1)}, u32[]{:S(2)}, u32[]{:S(2)}) collective-permute-start(f32[2,2,32,1024]{3,2,1,0:T(8,128)S(1)} %pad_maximum_fusion.7), channel_id=1, source_target_pairs={{0,24},{8,0},{16,8},{24,16},{32,56},{40,32},{48,40},{56,48},{1,25}... | collective-permute-start | bytes 1572872 | tf_op jit(solution)/shard_map/ppermute | solution.py:85
  408.3 12.1 %collective-permute-start.74 = (f32[2,32,256]{2,1,0:T(8,128)S(1)}, f32[2,32,256]{2,1,0:T(8,128)S(1)}, u32[]{:S(2)}, u32[]{:S(2)}) collective-permute-start(f32[2,32,256]{2,1,0:T(8,128)S(1)} %get-tuple-element.80), channel_id=1, source_target_pairs={{0,192},{64,128},{128,64},{192,0},{1,193},{65,129},{129,65},{193,1... | collective-permute-start | bytes 196616 | tf_op jit(solution)/shard_map/ppermute | solution.py:100
  (62 other events, 601.1 us)
